TPU v7x, 256 devices: a whole 4x4x8 slice. The times are simulated.
256 devices in a mesh: site: 2 (over core), wide: 32 (over x, z), narrow: 4 (over y).
Axes of the slice: x: 4, y: 4, z: 8, core: 2. Of those that a mesh axis runs over, the one named last changes fastest.
Arguments:
- initial_rows: float32 [64, 4, 2048], P('site', 'narrow'), may hold values from -6 to 6
- outcomes: int32 [64, 4], replicated, may hold values 0 or 1
- tensors: float32 [4, 2, 4, 2048, 8192], P('site', None, 'narrow', None, 'wide'), may hold values from -0.25 to 0.25
Outputs:
- final_rows: float32 [64, 4, 2048], P('site', 'narrow')
- log_weight: float32 [64], P('site')
All inputs are finite; a program needn't handle non-finite values.
Results may differ from a plain program's by a relative error of at most 0.0003.
Values sent between devices are 32-bit elements; how exact they have to be, the bound alone decides.
A program may use at most 64 MiB of HBM per device.

v0:
```python
import jax
import jax.numpy as jnp
from jax import lax
from jax.sharding import PartitionSpec as P

BOND = 8192
epsilon = 1e-06
highest = lax.Precision.HIGHEST


def from_partner(value, axis, distance):
    mask = 2**distance
    pairs = [(source, source ^ mask) for source in range(lax.axis_size(axis))]
    return lax.ppermute(value, axis, pairs)


def advance(held, log_sum, site_tensor, chosen):
    front = held.shape[0]
    groups = lax.axis_size("narrow")
    share = front // groups
    summed = lax.psum_scatter(
        jnp.einsum(
            "bar,oard->bod",
            held,
            site_tensor,
            precision=highest,
            preferred_element_type=jnp.float32,
        ),
        "narrow",
        scatter_dimension=0,
        tiled=True,
    )
    local_choice = lax.dynamic_slice_in_dim(chosen, lax.axis_index("narrow") * share, share, 0)
    squares = jnp.sum(summed * summed, axis=2)
    raw_kept = jnp.where(local_choice[:, None] == 0, summed[:, 0, :], summed[:, 1, :])
    totals = lax.psum(squares, "wide")
    both_mean = (totals[:, 0] + totals[:, 1]) / (2.0 * BOND)
    scale = lax.rsqrt(both_mean + epsilon)
    full_rows = lax.all_gather(raw_kept * scale[:, None], "wide", axis=1, tiled=True)
    kept_square = jnp.where(local_choice == 0, totals[:, 0], totals[:, 1])
    local_ratio = jnp.log(kept_square / BOND + epsilon) - jnp.log(both_mean + epsilon)
    ratio_table = jnp.broadcast_to(local_ratio[:, None], (share, groups))
    split_rows = full_rows.reshape(share, groups, -1)
    moved, moved_ratio = (
        lax.all_to_all(split_rows, "narrow", split_axis=1, concat_axis=0, tiled=True),
        lax.all_to_all(ratio_table, "narrow", split_axis=1, concat_axis=0, tiled=True),
    )
    return (moved, log_sum + moved_ratio[:, 0])


def run_section(held, log_sum, tensors, chosen_block):
    for local_site in range(tensors.shape[0]):
        held, log_sum = advance(held, log_sum, tensors[local_site], chosen_block[:, local_site])
    return (held, log_sum)


def hand_over(held, log_sum):
    moved_rows, moved_sum = from_partner((held, log_sum), "site", 0)
    return (moved_rows, moved_sum)


def shards(initial_rows, outcomes, tensors):
    section = lax.axis_index("site")
    front = initial_rows.shape[0]
    local_count = tensors.shape[0]
    section_columns = lax.dynamic_slice_in_dim(outcomes, section * local_count, local_count, 1)
    held = initial_rows
    log_sum = jnp.zeros((front,), jnp.float32)
    front_order = (section, 1 - section, section)
    for turn_index in range(3):
        new_rows, new_sum = run_section(
            held,
            log_sum,
            tensors,
            lax.dynamic_slice_in_dim(section_columns, front_order[turn_index] * front, front, 0),
        )
        if turn_index == 1:
            held, log_sum = (new_rows, new_sum)
        else:
            active = section == 0 if turn_index == 0 else section == 1
            held = jnp.where(active, new_rows, held)
            log_sum = jnp.where(active, new_sum, log_sum)
        if turn_index < 2:
            held, log_sum = hand_over(held, log_sum)
    return (held, log_sum)


def solution(mesh):
    placed = (P("site", "narrow", None), P(), P("site", None, "narrow", None, "wide"))
    return jax.shard_map(
        shards,
        mesh=mesh,
        in_specs=placed,
        out_specs=(P("site", "narrow", None), P("site")),
        check_vma=False,
    )
```

profile of v0, /device:TPU:2, one launch (start us, length us, event | category | flops | bytes accessed | tf_op | source)
XLA Modules:
  0.0 993.4 jit_solution(1777501969221541964)
XLA Ops:
  7.2 5.4 fusion.2
  12.7 0.8 fusion.33
  13.6 25.4 %reduce-scatter.7.cloned.1.call-done = f32[8,2,256]{2,0,1:T(8,128)} async-done(((f32[32,2,256]{2,0,1:T(8,128)}), f32[8,2,256]{2,0,1:T(8,128)}) %reduce-scatter.7.cloned.1.call-update) | async-done | bytes 16400 | tf_op jit(solution)/shard_map/reduce_scatter | solution.py:21
  39.0 0.8 multiply_reduce_fusion.5
  39.8 63.2 %psum.42 = f32[8,2]{0,1:T(2,128)S(1)} all-reduce(f32[8,2]{0,1:T(2,128)S(1)} %multiply_reduce_fusion.5), channel_id=1, replica_groups=mesh['site'=2,'wide'=32,'narrow'=4] {'wide'}, use_global_device_ids=true, to_apply=%region_2.3 | all-reduce | flops 16 | bytes 128 | tf_op jit(solution)/shard_map/psum | solution.py:36
  103.9 58.4 %all_gather.18 = f32[8,8192]{1,0:T(8,128)S(1)} all-gather(f32[8,256]{1,0:T(8,128)S(1)} %fusion.24), channel_id=1, replica_groups=mesh['site'=2,'wide'=32,'narrow'=4] {'wide'}, dimensions={1}, use_global_device_ids=true | all-gather | bytes 270336 | tf_op jit(solution)/shard_map/all_gather | solution.py:39
  162.3 9.2 all_to_all.171
  171.5 5.3 fusion.5
  176.9 18.2 %reduce-scatter.9.cloned.1.call-done = f32[8,2,256]{2,0,1:T(8,128)} async-done(((f32[32,2,256]{2,0,1:T(8,128)}), f32[8,2,256]{2,0,1:T(8,128)}) %reduce-scatter.9.cloned.1.call-update) | async-done | bytes 16400 | tf_op jit(solution)/shard_map/reduce_scatter | solution.py:21
  195.0 0.8 multiply_reduce_fusion.4
  195.9 63.2 %psum.43 = f32[8,2]{0,1:T(2,128)S(1)} all-reduce(f32[8,2]{0,1:T(2,128)S(1)} %multiply_reduce_fusion.4), channel_id=1, replica_groups=mesh['site'=2,'wide'=32,'narrow'=4] {'wide'}, use_global_device_ids=true, to_apply=%region_5.6 | all-reduce | flops 16 | bytes 128 | tf_op jit(solution)/shard_map/psum | solution.py:36
  260.0 62.4 %all_gather.19 = f32[8,8192]{1,0:T(8,128)} all-gather(f32[8,256]{1,0:T(8,128)S(1)} %fusion.22), channel_id=1, replica_groups=mesh['site'=2,'wide'=32,'narrow'=4] {'wide'}, dimensions={1}, use_global_device_ids=true | all-gather | bytes 270336 | tf_op jit(solution)/shard_map/all_gather | solution.py:39
  322.4 3.4 all-to-all-start.1
  325.9 6.6 all-to-all-done.1
  332.7 1.5 collective-permute-done
  334.2 5.3 fusion.1
  339.6 18.2 %reduce-scatter.11.cloned.1.call-done = f32[8,2,256]{2,0,1:T(8,128)} async-done(((f32[32,2,256]{2,0,1:T(8,128)}), f32[8,2,256]{2,0,1:T(8,128)}) %reduce-scatter.11.cloned.1.call-update) | async-done | bytes 16400 | tf_op jit(solution)/shard_map/reduce_scatter | solution.py:21
  357.8 0.8 multiply_reduce_fusion.3
  358.6 63.2 %psum.44 = f32[8,2]{0,1:T(2,128)S(1)} all-reduce(f32[8,2]{0,1:T(2,128)S(1)} %multiply_reduce_fusion.3), channel_id=1, replica_groups=mesh['site'=2,'wide'=32,'narrow'=4] {'wide'}, use_global_device_ids=true, to_apply=%region_8.9 | all-reduce | flops 16 | bytes 128 | tf_op jit(solution)/shard_map/psum | solution.py:36
  422.8 58.4 %all_gather.20 = f32[8,8192]{1,0:T(8,128)S(1)} all-gather(f32[8,256]{1,0:T(8,128)S(1)} %fusion.20), channel_id=1, replica_groups=mesh['site'=2,'wide'=32,'narrow'=4] {'wide'}, dimensions={1}, use_global_device_ids=true | all-gather | bytes 270336 | tf_op jit(solution)/shard_map/all_gather | solution.py:39
  481.1 9.2 all_to_all.172
  490.3 5.3 fusion.4
  495.7 18.1 %reduce-scatter.13.cloned.1.call-done = f32[8,2,256]{2,0,1:T(8,128)} async-done(((f32[32,2,256]{2,0,1:T(8,128)}), f32[8,2,256]{2,0,1:T(8,128)}) %reduce-scatter.13.cloned.1.call-update) | async-done | bytes 16400 | tf_op jit(solution)/shard_map/reduce_scatter | solution.py:21
  514.7 63.2 %psum.45 = f32[8,2]{0,1:T(2,128)S(1)} all-reduce(f32[8,2]{0,1:T(2,128)S(1)} %multiply_reduce_fusion.2), channel_id=1, replica_groups=mesh['site'=2,'wide'=32,'narrow'=4] {'wide'}, use_global_device_ids=true, to_apply=%region_11.12 | all-reduce | flops 16 | bytes 128 | tf_op jit(solution)/shard_map/psum | solution.py:36
  578.8 58.4 %all_gather.21 = f32[8,8192]{1,0:T(8,128)S(1)} all-gather(f32[8,256]{1,0:T(8,128)S(1)} %fusion.18), channel_id=1, replica_groups=mesh['site'=2,'wide'=32,'narrow'=4] {'wide'}, dimensions={1}, use_global_device_ids=true | all-gather | bytes 270336 | tf_op jit(solution)/shard_map/all_gather | solution.py:39
  637.2 9.2 all_to_all.173
  646.4 1.5 collective-permute-done.1
  647.9 5.3 fusion
  653.3 7.6 all_to_all.174
  661.5 3.2 all-to-all-start.7
  664.6 5.2 all-to-all-done.7
  670.0 1.4 reduce-scatter.15.cloned.1.call-done
  672.8 3.2 all-to-all-start.8
  676.0 63.3 %psum.46 = f32[8,2]{0,1:T(2,128)S(1)} all-reduce(f32[8,2]{0,1:T(2,128)S(1)} %multiply_reduce_fusion.1), channel_id=1, replica_groups=mesh['site'=2,'wide'=32,'narrow'=4] {'wide'}, use_global_device_ids=true, to_apply=%region_14.15 | all-reduce | flops 16 | bytes 128 | tf_op jit(solution)/shard_map/psum | solution.py:36
  740.7 4.7 all-to-all-start.9
  745.5 62.4 %all_gather.22 = f32[8,8192]{1,0:T(8,128)} all-gather(f32[8,256]{1,0:T(8,128)S(1)} %fusion.16), channel_id=1, replica_groups=mesh['site'=2,'wide'=32,'narrow'=4] {'wide'}, dimensions={1}, use_global_device_ids=true | all-gather | bytes 270336 | tf_op jit(solution)/shard_map/all_gather | solution.py:39
  807.9 4.8 all-to-all-start.4
  812.9 6.5 all-to-all-done.4
  819.4 5.3 fusion.3
  825.3 3.2 all-to-all-start.10
  828.6 5.1 all-to-all-done.10
  833.7 9.2 reduce-scatter.17.cloned.1.call-done
  843.8 63.2 %psum.47 = f32[8,2]{0,1:T(2,128)S(1)} all-reduce(f32[8,2]{0,1:T(2,128)S(1)} %multiply_reduce_fusion), channel_id=1, replica_groups=mesh['site'=2,'wide'=32,'narrow'=4] {'wide'}, use_global_device_ids=true, to_apply=%region_17.18 | all-reduce | flops 16 | bytes 128 | tf_op jit(solution)/shard_map/psum | solution.py:36
  907.7 3.2 all-to-all-start.11
  911.7 62.4 %all_gather.23 = f32[8,8192]{1,0:T(8,128)} all-gather(f32[8,256]{1,0:T(8,128)S(1)} %fusion.14), channel_id=1, replica_groups=mesh['site'=2,'wide'=32,'narrow'=4] {'wide'}, dimensions={1}, use_global_device_ids=true | all-gather | bytes 270336 | tf_op jit(solution)/shard_map/all_gather | solution.py:39
  974.1 4.8 all-to-all-start.5
  979.5 6.1 all-to-all-done.5
  985.6 1.0 copy.12
  (64 shorter events, 12.6 us)
Async XLA Ops:
  7.2 325.3 %copy-start = (f32[32,1,2048]{2,1,0:T(1,128)S(1)}, f32[32,1,2048]{2,1,0:T(1,128)}, u32[]{:S(2)}) copy-start(f32[32,1,2048]{2,1,0:T(1,128)} %param.3) | copy-start | bytes 786436
  7.2 31.8 %reduce-scatter.7.cloned.1.call-start = ((), (), s32[]{:S(2)}) async-start(), calls=%async_computation.18 | async-start | bytes 81920 | tf_op jit(solution)/shard_map/reduce_scatter | solution.py:21
  12.7 182.3 %reduce-scatter.9.cloned.1.call-start = ((), (), s32[]{:S(2)}) async-start(), calls=%async_computation.19 | async-start | bytes 81920 | tf_op jit(solution)/shard_map/reduce_scatter | solution.py:21
  322.4 10.1 %all-to-all-start.1 = ((f32[8,4,2048]{2,0,1:T(8,128)}), f32[8,4,2048]{2,0,1:T(8,128)S(1)}, u32[]{:S(2)}, u32[]{:S(2)}) async-start(f32[8,4,2048]{2,0,1:T(8,128)} %bitcast.19), calls=%async_computation.3 | async-start | bytes 524288 | tf_op jit(solution)/shard_map/all_to_all | solution.py:45
  325.8 31.9 %reduce-scatter.11.cloned.1.call-start = ((), (), s32[]{:S(2)}) async-start(), calls=%async_computation.20 | async-start | bytes 81920 | tf_op jit(solution)/shard_map/reduce_scatter | solution.py:21
  332.6 1.6 collective-permute-start
  339.5 174.3 %reduce-scatter.13.cloned.1.call-start = ((), (), s32[]{:S(2)}) async-start(), calls=%async_computation.21 | async-start | bytes 81920 | tf_op jit(solution)/shard_map/reduce_scatter | solution.py:21
  495.6 175.8 %reduce-scatter.15.cloned.1.call-start = ((), (), s32[]{:S(2)}) async-start(), calls=%async_computation.22 | async-start | bytes 81920 | tf_op jit(solution)/shard_map/reduce_scatter | solution.py:21
  646.4 1.5 collective-permute-start.1
  661.5 8.4 all-to-all-start.7
  670.0 154.7 %collective-permute-start.2 = (f32[32]{0:T(128)S(1)}, f32[32]{0:T(128)S(1)}, u32[]{:S(2)}, u32[]{:S(2)}) collective-permute-start(f32[32]{0:T(128)S(1)} %select_n.125), channel_id=1, source_target_pairs={{0,128},{128,0},{1,129},{129,1},{2,130},{130,2},{3,131},{131,3},{4... | collective-permute-start | bytes 392 | tf_op jit(solution)/shard_map/ppermute | solution.py:14
  672.8 67.4 %all-to-all-start.8 = ((f32[8,4,1]{0,2,1:T(1,128)}), f32[8,4,1]{0,2,1:T(1,128)S(1)}, u32[]{:S(2)}, u32[]{:S(2)}) async-start(f32[8,4,1]{0,2,1:T(1,128)} %broadcast_in_dim.99), calls=%async_computation.14 | async-start | bytes 4096 | tf_op jit(solution)/shard_map/all_to_all | solution.py:46
  740.7 67.1 %all-to-all-start.9 = ((f32[8,4,1]{0,2,1:T(1,128)}), f32[8,4,1]{0,2,1:T(1,128)S(1)}, u32[]{:S(2)}, u32[]{:S(2)}) async-start(f32[8,4,1]{0,2,1:T(1,128)} %broadcast_in_dim.100), calls=%async_computation.15 | async-start | bytes 4096 | tf_op jit(solution)/shard_map/all_to_all | solution.py:46
  807.9 11.5 %all-to-all-start.4 = ((f32[8,4,2048]{2,0,1:T(8,128)}), f32[8,4,2048]{2,0,1:T(8,128)S(1)}, u32[]{:S(2)}, u32[]{:S(2)}) async-start(f32[8,4,2048]{2,0,1:T(8,128)} %bitcast.45), calls=%async_computation.9 | async-start | bytes 524288 | tf_op jit(solution)/shard_map/all_to_all | solution.py:45
  812.7 30.3 %reduce-scatter.17.cloned.1.call-start = ((), (), s32[]{:S(2)}) async-start(), calls=%async_computation.23 | async-start | bytes 81920 | tf_op jit(solution)/shard_map/reduce_scatter | solution.py:21
  825.3 8.4 all-to-all-start.10
  828.5 150.6 %collective-permute-start.3 = (f32[32]{0:T(128)S(1)}, f32[32]{0:T(128)S(1)}, u32[]{:S(2)}, u32[]{:S(2)}) collective-permute-start(f32[32]{0:T(128)S(1)} %add_add_fusion), channel_id=1, source_target_pairs={{0,128},{128,0},{1,129},{129,1},{2,130},{130,2},{3,131},{131,3},{4... | collective-permute-start | bytes 392 | tf_op jit(solution)/shard_map/ppermute | solution.py:14
  907.7 66.4 %all-to-all-start.11 = ((f32[8,4,1]{0,2,1:T(1,128)}), f32[8,4,1]{0,2,1:T(1,128)S(1)}, u32[]{:S(2)}, u32[]{:S(2)}) async-start(f32[8,4,1]{0,2,1:T(1,128)} %broadcast_in_dim.102), calls=%async_computation.17 | async-start | bytes 4096 | tf_op jit(solution)/shard_map/all_to_all | solution.py:46
  974.1 11.4 %all-to-all-start.5 = ((f32[8,4,2048]{2,0,1:T(8,128)}), f32[8,4,2048]{2,0,1:T(8,128)S(1)}, u32[]{:S(2)}, u32[]{:S(2)}) async-start(f32[8,4,2048]{2,0,1:T(8,128)} %bitcast.53), calls=%async_computation.11 | async-start | bytes 524288 | tf_op jit(solution)/shard_map/all_to_all | solution.py:45
Sparse Core Ops, SparseCore 0:
  12.8 26.1 reduce-scatter.6
  177.0 18.0 reduce-scatter.8
  339.6 18.0 reduce-scatter.10
  495.8 18.0 reduce-scatter.12
  653.4 18.0 reduce-scatter.14
  824.8 18.0 reduce-scatter.16
where the time goes:
time: 995 us; the launch traced here: 993 us
  blocking collectives  777 us (78%)
  waiting for transfers between devices  123 us (12%)
  matrix products  31.9 us (3%)
  starting transfers between devices  30.9 us (3%)
  between operations  14.3 us (1%)
  other arithmetic  11 us (1%)
    psum x6, blocking collectives, advance(): totals = lax.psum(squares, 'wide')  379 us
    all_gather x6, blocking collectives, advance(): lax.all_gather(raw_kept * scale[:, None], 'wide', axis=1, tiled=True)  362 us
    reduce_scatter x6, waiting for transfers between devices, advance(): lax.psum_scatter(jnp.einsum('bar,oard->bod', held, site_tensor, precision...  90.4 us
    dot_general x6, matrix products, advance(): jnp.einsum('bar,oard->bod', held, site_tensor, precision=highest, preferr...  31.9 us
    all_to_all x3, blocking collectives, advance(): lax.all_to_all(split_rows, 'narrow', split_axis=1, concat_axis=0, tiled=T...  27.6 us
  transfers between devices with their start and end apart: 18, of which 13 were waited for; matrix products, arithmetic and copies ran while one was open for 1% of the time, Pallas kernels for 0%

commit v1 on v0

--- a/solution.py
+++ b/solution.py
@@ -1,3 +1,4 @@
+import functools
 import jax
 import jax.numpy as jnp
 from jax import lax
@@ -6,6 +7,19 @@
 BOND = 8192
 epsilon = 1e-06
 highest = lax.Precision.HIGHEST
+
+
+def produce_column(raw, across, d0, row_dim):
+    block_out = jax.lax.all_to_all(
+        jnp.stack(jnp.split(raw, jax.lax.axis_size(across), axis=d0)),
+        axis_name=across,
+        split_axis=0,
+        concat_axis=0,
+    )
+    return jnp.concatenate(block_out, axis=row_dim)
+
+
+group_search = functools.partial(produce_column, across="narrow", d0=1, row_dim=0)
 
 
 def from_partner(value, axis, distance):
@@ -42,7 +56,7 @@
     ratio_table = jnp.broadcast_to(local_ratio[:, None], (share, groups))
     split_rows = full_rows.reshape(share, groups, -1)
     moved, moved_ratio = (
-        lax.all_to_all(split_rows, "narrow", split_axis=1, concat_axis=0, tiled=True),
+        group_search(split_rows),
         lax.all_to_all(ratio_table, "narrow", split_axis=1, concat_axis=0, tiled=True),
     )
     return (moved, log_sum + moved_ratio[:, 0])

time: 995 us -> 989 us (level)
  blocking collectives: 777 us -> 765 us
    all_gather x6, blocking collectives: 362 us -> 350 us  [advance(): lax.all_gather(raw_kept * scale[:, None], 'wide', axis=1, tiled=True)]
  transfers between devices with their start and end apart: 18 -> 18, of which waited for: 13 -> 14; matrix products, arithmetic and copies ran while one was open for 1% -> 2% of each run, Pallas kernels for 0% -> 0%
where the time goes in v1:
time: 989 us; the launch traced here: 987 us
  blocking collectives  765 us (77%)
  waiting for transfers between devices  127 us (13%)
  matrix products  31.9 us (3%)
  starting transfers between devices  29.5 us (3%)
  between operations  14.4 us (1%)
  other arithmetic  13.2 us (1%)
    psum x6, blocking collectives, advance(): totals = lax.psum(squares, 'wide')  379 us
    all_gather x6, blocking collectives, advance(): lax.all_gather(raw_kept * scale[:, None], 'wide', axis=1, tiled=True)  350 us
    reduce_scatter x6, waiting for transfers between devices, advance(): lax.psum_scatter(jnp.einsum('bar,oard->bod', held, site_tensor, precision...  90.3 us
    dot_general x6, matrix products, advance(): jnp.einsum('bar,oard->bod', held, site_tensor, precision=highest, preferr...  31.9 us
    all_to_all x3, blocking collectives, produce_column(): jax.lax.all_to_all(jnp.stack(jnp.split(raw, jax.lax.axis_size(across), ax...  27.6 us
  transfers between devices with their start and end apart: 18, of which 14 were waited for; matrix products, arithmetic and copies ran while one was open for 2% of the time, Pallas kernels for 0%

profile of v1, /device:TPU:2, one launch (start us, length us, event | category | flops | bytes accessed | tf_op | source)
XLA Modules:
  0.0 986.6 jit_solution(17648327281878155536)
XLA Ops:
  7.2 5.4 fusion.2
  12.7 0.8 fusion.33
  13.6 25.4 %reduce-scatter.7.cloned.1.call-done = f32[8,2,256]{2,0,1:T(8,128)} async-done(((f32[32,2,256]{2,0,1:T(8,128)}), f32[8,2,256]{2,0,1:T(8,128)}) %reduce-scatter.7.cloned.1.call-update) | async-done | bytes 16400 | tf_op jit(solution)/shard_map/reduce_scatter | solution.py:35
  39.0 0.8 multiply_reduce_fusion.5
  39.8 63.2 %psum.42 = f32[8,2]{0,1:T(2,128)S(1)} all-reduce(f32[8,2]{0,1:T(2,128)S(1)} %multiply_reduce_fusion.5), channel_id=1, replica_groups=mesh['site'=2,'wide'=32,'narrow'=4] {'wide'}, use_global_device_ids=true, to_apply=%region_2.3 | all-reduce | flops 16 | bytes 128 | tf_op jit(solution)/shard_map/psum | solution.py:50
  103.9 58.4 %all_gather.18 = f32[8,8192]{1,0:T(8,128)S(1)} all-gather(f32[8,256]{1,0:T(8,128)S(1)} %fusion.24), channel_id=1, replica_groups=mesh['site'=2,'wide'=32,'narrow'=4] {'wide'}, dimensions={1}, use_global_device_ids=true | all-gather | bytes 270336 | tf_op jit(solution)/shard_map/all_gather | solution.py:53
  162.4 9.2 all_to_all.102
  171.6 5.3 fusion.5
  176.9 18.2 %reduce-scatter.9.cloned.1.call-done = f32[8,2,256]{2,0,1:T(8,128)} async-done(((f32[32,2,256]{2,0,1:T(8,128)}), f32[8,2,256]{2,0,1:T(8,128)}) %reduce-scatter.9.cloned.1.call-update) | async-done | bytes 16400 | tf_op jit(solution)/shard_map/reduce_scatter | solution.py:35
  195.1 0.8 multiply_reduce_fusion.4
  196.0 63.2 %psum.43 = f32[8,2]{0,1:T(2,128)S(1)} all-reduce(f32[8,2]{0,1:T(2,128)S(1)} %multiply_reduce_fusion.4), channel_id=1, replica_groups=mesh['site'=2,'wide'=32,'narrow'=4] {'wide'}, use_global_device_ids=true, to_apply=%region_5.6 | all-reduce | flops 16 | bytes 128 | tf_op jit(solution)/shard_map/psum | solution.py:50
  260.1 58.4 %all_gather.19 = f32[8,8192]{1,0:T(8,128)S(1)} all-gather(f32[8,256]{1,0:T(8,128)S(1)} %fusion.22), channel_id=1, replica_groups=mesh['site'=2,'wide'=32,'narrow'=4] {'wide'}, dimensions={1}, use_global_device_ids=true | all-gather | bytes 270336 | tf_op jit(solution)/shard_map/all_gather | solution.py:53
  319.2 3.4 all-to-all-start.1
  322.7 6.6 all-to-all-done.1
  329.5 1.5 collective-permute-done
  331.0 5.3 fusion.1
  336.4 18.1 %reduce-scatter.11.cloned.1.call-done = f32[8,2,256]{2,0,1:T(8,128)} async-done(((f32[32,2,256]{2,0,1:T(8,128)}), f32[8,2,256]{2,0,1:T(8,128)}) %reduce-scatter.11.cloned.1.call-update) | async-done | bytes 16400 | tf_op jit(solution)/shard_map/reduce_scatter | solution.py:35
  355.3 63.2 %psum.44 = f32[8,2]{0,1:T(2,128)S(1)} all-reduce(f32[8,2]{0,1:T(2,128)S(1)} %multiply_reduce_fusion.3), channel_id=1, replica_groups=mesh['site'=2,'wide'=32,'narrow'=4] {'wide'}, use_global_device_ids=true, to_apply=%region_8.9 | all-reduce | flops 16 | bytes 128 | tf_op jit(solution)/shard_map/psum | solution.py:50
  419.4 58.4 %all_gather.20 = f32[8,8192]{1,0:T(8,128)S(1)} all-gather(f32[8,256]{1,0:T(8,128)S(1)} %fusion.20), channel_id=1, replica_groups=mesh['site'=2,'wide'=32,'narrow'=4] {'wide'}, dimensions={1}, use_global_device_ids=true | all-gather | bytes 270336 | tf_op jit(solution)/shard_map/all_gather | solution.py:53
  477.9 9.2 all_to_all.103
  487.1 5.3 fusion.4
  492.5 18.1 %reduce-scatter.13.cloned.1.call-done = f32[8,2,256]{2,0,1:T(8,128)} async-done(((f32[32,2,256]{2,0,1:T(8,128)}), f32[8,2,256]{2,0,1:T(8,128)}) %reduce-scatter.13.cloned.1.call-update) | async-done | bytes 16400 | tf_op jit(solution)/shard_map/reduce_scatter | solution.py:35
  511.5 63.2 %psum.45 = f32[8,2]{0,1:T(2,128)S(1)} all-reduce(f32[8,2]{0,1:T(2,128)S(1)} %multiply_reduce_fusion.2), channel_id=1, replica_groups=mesh['site'=2,'wide'=32,'narrow'=4] {'wide'}, use_global_device_ids=true, to_apply=%region_11.12 | all-reduce | flops 16 | bytes 128 | tf_op jit(solution)/shard_map/psum | solution.py:50
  575.6 58.4 %all_gather.21 = f32[8,8192]{1,0:T(8,128)S(1)} all-gather(f32[8,256]{1,0:T(8,128)S(1)} %fusion.18), channel_id=1, replica_groups=mesh['site'=2,'wide'=32,'narrow'=4] {'wide'}, dimensions={1}, use_global_device_ids=true | all-gather | bytes 270336 | tf_op jit(solution)/shard_map/all_gather | solution.py:53
  634.0 9.2 all_to_all.104
  643.2 1.5 collective-permute-done.1
  644.7 5.3 fusion
  650.1 7.6 all_to_all.105
  658.3 3.2 all-to-all-start.7
  661.4 5.2 all-to-all-done.7
  666.8 1.4 reduce-scatter.15.cloned.1.call-done
  669.6 3.2 all-to-all-start.8
  672.8 63.3 %psum.46 = f32[8,2]{0,1:T(2,128)S(1)} all-reduce(f32[8,2]{0,1:T(2,128)S(1)} %multiply_reduce_fusion.1), channel_id=1, replica_groups=mesh['site'=2,'wide'=32,'narrow'=4] {'wide'}, use_global_device_ids=true, to_apply=%region_14.15 | all-reduce | flops 16 | bytes 128 | tf_op jit(solution)/shard_map/psum | solution.py:50
  737.0 58.4 %all_gather.22 = f32[8,8192]{1,0:T(8,128)S(1)} all-gather(f32[8,256]{1,0:T(8,128)S(1)} %fusion.16), channel_id=1, replica_groups=mesh['site'=2,'wide'=32,'narrow'=4] {'wide'}, dimensions={1}, use_global_device_ids=true | all-gather | bytes 270336 | tf_op jit(solution)/shard_map/all_gather | solution.py:53
  796.0 4.7 all-to-all-start.9
  801.4 4.4 all-to-all-done.9
  805.8 3.4 all-to-all-start.4
  809.5 6.4 all-to-all-done.4
  815.9 5.3 fusion.3
  821.8 3.2 all-to-all-start.10
  825.1 5.1 all-to-all-done.10
  830.3 9.1 reduce-scatter.17.cloned.1.call-done
  840.3 63.2 %psum.47 = f32[8,2]{0,1:T(2,128)S(1)} all-reduce(f32[8,2]{0,1:T(2,128)S(1)} %multiply_reduce_fusion), channel_id=1, replica_groups=mesh['site'=2,'wide'=32,'narrow'=4] {'wide'}, use_global_device_ids=true, to_apply=%region_17.18 | all-reduce | flops 16 | bytes 128 | tf_op jit(solution)/shard_map/psum | solution.py:50
  904.2 3.2 all-to-all-start.11
  908.1 58.4 %all_gather.23 = f32[8,8192]{1,0:T(8,128)S(1)} all-gather(f32[8,256]{1,0:T(8,128)S(1)} %fusion.14), channel_id=1, replica_groups=mesh['site'=2,'wide'=32,'narrow'=4] {'wide'}, dimensions={1}, use_global_device_ids=true | all-gather | bytes 270336 | tf_op jit(solution)/shard_map/all_gather | solution.py:53
  967.3 4.8 all-to-all-start.5
  972.7 6.1 all-to-all-done.5
  978.7 1.0 copy.12
  (76 shorter events, 15.8 us)
Async XLA Ops:
  7.2 322.1 %copy-start = (f32[32,1,2048]{2,1,0:T(1,128)S(1)}, f32[32,1,2048]{2,1,0:T(1,128)}, u32[]{:S(2)}) copy-start(f32[32,1,2048]{2,1,0:T(1,128)} %param.3) | copy-start | bytes 786436
  7.2 31.8 %reduce-scatter.7.cloned.1.call-start = ((), (), s32[]{:S(2)}) async-start(), calls=%async_computation.18 | async-start | bytes 81920 | tf_op jit(solution)/shard_map/reduce_scatter | solution.py:35
  12.7 182.4 %reduce-scatter.9.cloned.1.call-start = ((), (), s32[]{:S(2)}) async-start(), calls=%async_computation.19 | async-start | bytes 81920 | tf_op jit(solution)/shard_map/reduce_scatter | solution.py:35
  319.2 10.1 %all-to-all-start.1 = ((f32[4,8,1,2048]{3,1,2,0:T(8,128)}), f32[4,8,1,2048]{3,1,2,0:T(8,128)S(1)}, u32[]{:S(2)}, u32[]{:S(2)}) async-start(f32[4,8,1,2048]{3,1,2,0:T(8,128)} %pad_maximum_fusion.1), calls=%async_computation.3 | async-start | bytes 524288 | tf_op jit(solution)/shard_map/all_to_all | solution.py:13
  322.6 31.9 %reduce-scatter.11.cloned.1.call-start = ((), (), s32[]{:S(2)}) async-start(), calls=%async_computation.20 | async-start | bytes 81920 | tf_op jit(solution)/shard_map/reduce_scatter | solution.py:35
  329.4 1.6 collective-permute-start
  336.3 174.3 %reduce-scatter.13.cloned.1.call-start = ((), (), s32[]{:S(2)}) async-start(), calls=%async_computation.21 | async-start | bytes 81920 | tf_op jit(solution)/shard_map/reduce_scatter | solution.py:35
  492.4 175.8 %reduce-scatter.15.cloned.1.call-start = ((), (), s32[]{:S(2)}) async-start(), calls=%async_computation.22 | async-start | bytes 81920 | tf_op jit(solution)/shard_map/reduce_scatter | solution.py:35
  643.2 1.5 collective-permute-start.1
  658.3 8.4 all-to-all-start.7
  666.8 154.4 %collective-permute-start.2 = (f32[32]{0:T(128)S(1)}, f32[32]{0:T(128)S(1)}, u32[]{:S(2)}, u32[]{:S(2)}) collective-permute-start(f32[32]{0:T(128)S(1)} %select_n.125), channel_id=1, source_target_pairs={{0,128},{128,0},{1,129},{129,1},{2,130},{130,2},{3,131},{131,3},{4... | collective-permute-start | bytes 392 | tf_op jit(solution)/shard_map/ppermute | solution.py:28
  669.6 125.8 %all-to-all-start.8 = ((f32[8,4,1]{0,2,1:T(1,128)}), f32[8,4,1]{0,2,1:T(1,128)S(1)}, u32[]{:S(2)}, u32[]{:S(2)}) async-start(f32[8,4,1]{0,2,1:T(1,128)} %broadcast_in_dim.99), calls=%async_computation.14 | async-start | bytes 4096 | tf_op jit(solution)/shard_map/all_to_all | solution.py:60
  796.0 9.9 %all-to-all-start.9 = ((f32[8,4,1]{0,2,1:T(1,128)}), f32[8,4,1]{0,2,1:T(1,128)S(1)}, u32[]{:S(2)}, u32[]{:S(2)}) async-start(f32[8,4,1]{0,2,1:T(1,128)} %broadcast_in_dim.100), calls=%async_computation.15 | async-start | bytes 4096 | tf_op jit(solution)/shard_map/all_to_all | solution.py:60
  805.8 10.1 %all-to-all-start.4 = ((f32[4,8,1,2048]{3,1,2,0:T(8,128)}), f32[4,8,1,2048]{3,1,2,0:T(8,128)S(1)}, u32[]{:S(2)}, u32[]{:S(2)}) async-start(f32[4,8,1,2048]{3,1,2,0:T(8,128)} %pad_maximum_fusion.4), calls=%async_computation.9 | async-start | bytes 524288 | tf_op jit(solution)/shard_map/all_to_all | solution.py:13
  809.3 30.1 %reduce-scatter.17.cloned.1.call-start = ((), (), s32[]{:S(2)}) async-start(), calls=%async_computation.23 | async-start | bytes 81920 | tf_op jit(solution)/shard_map/reduce_scatter | solution.py:35
  821.8 8.4 all-to-all-start.10
  825.0 147.1 %collective-permute-start.3 = (f32[32]{0:T(128)S(1)}, f32[32]{0:T(128)S(1)}, u32[]{:S(2)}, u32[]{:S(2)}) collective-permute-start(f32[32]{0:T(128)S(1)} %add_add_fusion), channel_id=1, source_target_pairs={{0,128},{128,0},{1,129},{129,1},{2,130},{130,2},{3,131},{131,3},{4... | collective-permute-start | bytes 392 | tf_op jit(solution)/shard_map/ppermute | solution.py:28
  904.2 63.1 %all-to-all-start.11 = ((f32[8,4,1]{0,2,1:T(1,128)}), f32[8,4,1]{0,2,1:T(1,128)S(1)}, u32[]{:S(2)}, u32[]{:S(2)}) async-start(f32[8,4,1]{0,2,1:T(1,128)} %broadcast_in_dim.102), calls=%async_computation.17 | async-start | bytes 4096 | tf_op jit(solution)/shard_map/all_to_all | solution.py:60
  967.3 11.4 %all-to-all-start.5 = ((f32[4,8,1,2048]{3,1,2,0:T(8,128)}), f32[4,8,1,2048]{3,1,2,0:T(8,128)S(1)}, u32[]{:S(2)}, u32[]{:S(2)}) async-start(f32[4,8,1,2048]{3,1,2,0:T(8,128)} %pad_maximum_fusion.5), calls=%async_computation.11 | async-start | bytes 524288 | tf_op jit(solution)/shard_map/all_to_all | solution.py:13
Sparse Core Ops, SparseCore 0:
  12.8 26.1 reduce-scatter.6
  177.0 18.0 reduce-scatter.8
  336.4 18.0 reduce-scatter.10
  492.5 18.0 reduce-scatter.12
  650.2 18.0 reduce-scatter.14
  821.3 18.0 reduce-scatter.16
